TPU v7x, 32 devices: a whole 2x2x4 slice. The times are simulated.
32 devices in a mesh: grp: 2 (over x), region: 8 (over z, y), donor: 2 (over core).
Axes of the slice: x: 2, y: 2, z: 4, core: 2. Of those that a mesh axis runs over, the one named last changes fastest.
Arguments:
- dosage: bfloat16 [16384, 8192], P(('grp', 'region'), 'donor'), parts along dimension 0, may hold values from 0 to 2, as said below
- expression: bfloat16 [512, 8192], P(('grp', 'region'), 'donor'), parts along dimension 0, may hold values from -60 to 60
- cis_tiles: int32 [512, 8], P(('grp', 'region')), parts along dimension 0, may hold values from 0 to 63, as said below
Outputs:
- correlation: float32 [512, 1024], P(('grp', 'region'), 'donor'), parts along dimension 0
- pvalue: float32 [512, 1024], P(('grp', 'region'), 'donor'), parts along dimension 0
There are 2 independent parts, one for each index of `grp`. A program takes and returns all parts, laid end to end along the dimension named above; each array names one. Nothing has to cross between parts.
Inputs may be any that keep to these rules, and one draw needn't show every extreme that they name: `dosage`: imputed dosages, within the bounds. `cis_tiles`: each gene's 8 cis tiles are consecutive tile numbers; for the genes of region block r (rows r * 32 to (r + 1) * 32 - 1) they lie from r * 8 - 8 to (r + 1) * 8 + 7, and both ends are reached in every block where they exist.
All inputs are finite; a program needn't handle non-finite values.
Results may differ from a plain program's by a relative error of at most 0.0044.
Values may be sent and summed in bfloat16 or wider, within the bound.
A program may use at most 128 MiB of HBM per device.

v0:
```python
import math
import jax
import jax.numpy as jnp
from jax import lax
from jax.sharding import PartitionSpec as P

TILE = 128
RIM = 8
CF_TERMS = 32


def with_halo(array, sides, width):
    for axis, dim in sides:
        count, length = (lax.axis_size(axis), array.shape[dim])
        up = [(i, (i + 1) % count) for i in range(count - 1)]
        down = [(j, i) for i, j in up]
        last = lax.slice_in_dim(array, length - width, length, axis=dim)
        leading = lax.slice_in_dim(array, 0, width, axis=dim)
        before = lax.ppermute(last, axis, up)
        after = lax.ppermute(leading, axis, down)
        array = jnp.concatenate([before, array, after], axis=dim)
    return array


def beta_log_constant(shape_a):
    inverse = 1.0 / shape_a
    ratio = (
        0.5 * math.log(shape_a)
        - inverse / 8.0
        + inverse**3 / 192.0
        + inverse**5 / 640.0
        - 17.0 * inverse**7 / 14336.0
    )
    return ratio - 0.5 * math.log(math.pi)


def scale_rows(values, totals, squares, count):
    center = totals / count
    spread = squares / count - center * center
    return (
        (values.astype(jnp.float32) - center[:, None]) * lax.rsqrt(spread + 1e-05)[:, None]
    ).astype(jnp.bfloat16)


def donor_product(left_rows, right_rows):
    return lax.dot_general(
        left_rows, right_rows, (((1,), (1,)), ((), ())), preferred_element_type=jnp.float32
    )


def tail_probability(squared, shape_a, log_const, terms):
    narrow = squared < 1.5 / (shape_a + 2.5)
    first = jnp.where(narrow, 0.5, shape_a)
    second = jnp.where(narrow, shape_a, 0.5)
    argument = jnp.where(narrow, squared, 1.0 - squared)
    total_ab = first + second

    def odd_term(index):
        return (
            -(first + index)
            * (total_ab + index)
            * argument
            / ((first + 2.0 * index) * (first + 2.0 * index + 1.0))
        )

    def even_term(index):
        return (
            index
            * (second - index)
            * argument
            / ((first + 2.0 * index - 1.0) * (first + 2.0 * index))
        )

    def advance(carried, coefficient):
        upper_ratio, lower_ratio, estimate = carried
        lower_ratio = 1.0 / (1.0 + coefficient * lower_ratio)
        upper_ratio = 1.0 + coefficient / upper_ratio
        return (upper_ratio, lower_ratio, estimate * lower_ratio * upper_ratio)

    def sweep(turn, carried):
        for offset in range(4):
            index = (4 * turn + offset + 1).astype(jnp.float32)
            carried = advance(carried, even_term(index))
            carried = advance(carried, odd_term(index))
        return carried

    leading = 1.0 / (1.0 - total_ab * argument / (first + 1.0))
    start = (jnp.ones_like(squared), leading, leading)
    carried = lax.fori_loop(0, terms // 4, sweep, start)
    estimate = carried[2]
    front = jnp.sqrt(squared) * jnp.exp(shape_a * jnp.log1p(-squared) + log_const)
    share = front * estimate / first
    return jnp.where(narrow, 1.0 - share, share)


def shards(dosage, expression, cis_tiles):
    donor_total = dosage.shape[1] * lax.axis_size("donor")
    gene_count = expression.shape[0]
    block_tiles = dosage.shape[0] // TILE
    rim_rows = RIM * TILE
    dose_total = jnp.sum(dosage, axis=1, dtype=jnp.float32)
    dose_square = jnp.sum(jnp.square(dosage.astype(jnp.float32)), axis=1)
    expr_total = jnp.sum(expression, axis=1, dtype=jnp.float32)
    expr_square = jnp.sum(jnp.square(expression.astype(jnp.float32)), axis=1)
    moments = lax.psum((dose_total, dose_square, expr_total, expr_square), "donor")
    zdose = scale_rows(dosage, moments[0], moments[1], donor_total)
    zexpr = scale_rows(expression, moments[2], moments[3], donor_total)
    widened = with_halo(zdose, (("region", 0),), rim_rows)
    dense = donor_product(zexpr, widened)
    first_tile = lax.axis_index("region") * block_tiles - RIM
    local_tile = cis_tiles - first_tile
    layered = dense.reshape(gene_count, block_tiles + 2 * RIM, TILE)
    index_grid = jnp.broadcast_to(local_tile[:, :, None], (gene_count, local_tile.shape[1], TILE))
    picked = jnp.take_along_axis(layered, index_grid, axis=1)
    partial_pairs = picked.reshape(gene_count, local_tile.shape[1] * TILE)
    share_width = partial_pairs.shape[1] // lax.axis_size("donor")
    summed = lax.psum(partial_pairs, "donor")
    own_pairs = lax.dynamic_slice_in_dim(
        summed, lax.axis_index("donor") * share_width, share_width, 1
    )
    correlation = own_pairs / donor_total
    squared = jnp.minimum(correlation * correlation, 0.9)
    shape_a = (donor_total - 2) / 2.0
    log_const = beta_log_constant(shape_a)
    pvalue = tail_probability(squared, shape_a, log_const, CF_TERMS)
    return (correlation, pvalue)


def solution(mesh):
    in_specs = (
        P(("grp", "region"), "donor"),
        P(("grp", "region"), "donor"),
        P(("grp", "region"), None),
    )
    out_specs = (P(("grp", "region"), "donor"), P(("grp", "region"), "donor"))
    return jax.shard_map(shards, mesh=mesh, in_specs=in_specs, out_specs=out_specs, check_vma=False)
```

profile of v0, /device:TPU:0, one launch (start us, length us, event | category | flops | bytes accessed | tf_op | source)
XLA Modules:
  0.0 695.8 jit_solution(16506730900923522625)
XLA Ops:
  7.2 6.0 convert_reduce_fusion
  13.2 0.2 convert_reduce_fusion.1
  13.4 2.6 all-reduce
  16.1 11.0 %fusion.9 = bf16[1024,4096]{1,0:T(8,128)(2,1)} fusion(bf16[1024,4096]{1,0:T(8,128)(2,1)} %param.5, f32[1024]{0:T(1024)S(1)} %get-tuple-element.298, f32[1024]{0:T(1024)S(1)} %get-tuple-element.297), kind=kLoop, calls=%fused_computation.46 | loop fusion | flops 16777216 | bytes 16785408 | tf_op jit(solution)/shard_map/convert_element_type | solution.py:42
  27.1 8.0 %collective-permute-start = (bf16[1024,4096]{1,0:T(8,128)(2,1)}, bf16[1024,4096]{1,0:T(8,128)(2,1)}, u32[]{:S(2)}, u32[]{:S(2)}) collective-permute-start(bf16[1024,4096]{1,0:T(8,128)(2,1)} %fusion.9), channel_id=1, source_target_pairs={{0,2},{2,4},{4,6},{6,8},{8,10},{10,12},{12,14},{1,3},{3,5},{5,7},{... | collective-permute-start | bytes 25165832 | tf_op jit(solution)/shard_map/ppermute | solution.py:19
  35.0 1.3 collective-permute-start.1
  36.6 0.2 or_bitcast_fusion
  36.8 355.1 %collective-permute-done = bf16[1024,4096]{1,0:T(8,128)(2,1)} collective-permute-done((bf16[1024,4096]{1,0:T(8,128)(2,1)}, bf16[1024,4096]{1,0:T(8,128)(2,1)}, u32[]{:S(2)}, u32[]{:S(2)}) %collective-permute-start) | collective-permute-done | bytes 8388640 | tf_op jit(solution)/shard_map/ppermute | solution.py:19
  391.9 11.8 %fusion.11 = f32[4,8,24,128]{3,1,2,0:T(8,128)S(1)} fusion(bf16[1024,4096]{1,0:T(8,128)(2,1)} %collective-permute-done.1, bf16[1024,4096]{1,0:T(8,128)(2,1)} %fusion.9, bf16[1024,4096]{1,0:T(8,128)(2,1)} %collective-permute-done, bf16[32,4096]{1,0:T(8,128)(2,1)S(1)} %copy-done.1, f32[32]{0:T(128)S(1)} %get-tuple-element.300, f32[32]{0:T(128)S(1)} %get-tuple-element.299), kind=kOutput, calls=%fused_computation.48 | convolution fusion | flops 881328128 | bytes 25821440 | tf_op jit(solution)/shard_map/dot_general | solution.py:46
  403.8 259.4 %gather_fusion = f32[32768]{0:T(1024)S(1)} fusion(f32[32,24,128]{2,1,0:T(8,128)S(1)} %bitcast.11, s32[32768]{0:T(1024)S(1)} %or_bitcast_fusion), kind=kCustom, calls=%fused_computation | custom fusion | bytes 655360 | tf_op jit(solution)/shard_map/jit(take_along_axis)/gather | solution.py:114
  663.2 0.2 bitcast_select_fusion
  663.4 0.7 copy.20
  664.1 20.2 %all-reduce.3.cloned.1.call-done = f32[32,1024]{1,0:T(8,128)} async-done(((f32[32,1024]{1,0:T(8,128)}), f32[32,1024]{1,0:T(8,128)}) %all-reduce.3.cloned.1.call-update) | async-done | bytes 131088 | tf_op jit(solution)/shard_map/psum | solution.py:117
  684.3 0.9 broadcast_select_fusion
  685.3 3.0 while.21
  685.3 0.3 multiply_multiply_fusion.10
  685.7 0.3 multiply_multiply_fusion.10
  686.0 0.3 multiply_multiply_fusion.10
  686.4 0.3 multiply_multiply_fusion.10
  686.8 0.3 multiply_multiply_fusion.10
  687.2 0.3 multiply_multiply_fusion.10
  687.5 0.3 multiply_multiply_fusion.10
  687.9 0.3 multiply_multiply_fusion.10
  688.2 0.7 subtract_select_fusion
  (20 shorter events, 0.5 us)
Async XLA Ops:
  7.2 6.0 copy-start.1
  7.2 677.1 %all-reduce.3.cloned.1.call-start = ((), (), s32[]{:S(2)}) async-start(), calls=%async_computation | async-start | bytes 262144 | tf_op jit(solution)/shard_map/psum | solution.py:117
  16.0 20.3 %copy-start.2 = (s32[32,8]{0,1:T(8,128)S(1)}, s32[32,8]{0,1:T(8,128)}, u32[]{:S(2)}) copy-start(s32[32,8]{0,1:T(8,128)} %param.7) | copy-start | bytes 3076
  27.1 364.8 %collective-permute-start = (bf16[1024,4096]{1,0:T(8,128)(2,1)}, bf16[1024,4096]{1,0:T(8,128)(2,1)}, u32[]{:S(2)}, u32[]{:S(2)}) collective-permute-start(bf16[1024,4096]{1,0:T(8,128)(2,1)} %fusion.9), channel_id=1, source_target_pairs={{0,2},{2,4},{4,6},{6,8},{8,10},{10,12},{12,14},{1,3},{3,5},{5,7},{... | collective-permute-start | bytes 25165832 | tf_op jit(solution)/shard_map/ppermute | solution.py:19
  35.0 356.9 %collective-permute-start.1 = (bf16[1024,4096]{1,0:T(8,128)(2,1)}, bf16[1024,4096]{1,0:T(8,128)(2,1)}, u32[]{:S(2)}, u32[]{:S(2)}) collective-permute-start(bf16[1024,4096]{1,0:T(8,128)(2,1)} %fusion.9), channel_id=1, source_target_pairs={{2,0},{4,2},{6,4},{8,6},{10,8},{12,10},{14,12},{3,1},{5,3},{7,5},{... | collective-permute-start | bytes 25165832 | tf_op jit(solution)/shard_map/ppermute | solution.py:20
  685.2 3.8 copy-start
Sparse Core Ops, SparseCore 0:
  664.2 20.0 all-reduce.2
where the time goes:
time: 696 us
  waiting for transfers between devices  375 us (54%)
  local copies, waits for them, and re-layouts  260 us (37%)
  other arithmetic  21.9 us (3%)
  between operations  14.2 us (2%)
  matrix products  11.8 us (2%)
  starting transfers between devices  9.27 us (1%)
    ppermute x1, waiting for transfers between devices, with_halo(): before = lax.ppermute(last, axis, up)  355 us
    gather x1, local copies, waits for them, and re-layouts, shards(): picked = jnp.take_along_axis(layered, index_grid, axis=1)  259 us
    psum x1, waiting for transfers between devices, shards(): summed = lax.psum(partial_pairs, 'donor')  20.2 us
  transfers between devices with their start and end apart: 3, of which 2 were waited for; matrix products, arithmetic and copies ran while one was open for 0% of the time, Pallas kernels for 0%

commit v1 on v0

--- a/solution.py
+++ b/solution.py
@@ -3,6 +3,7 @@
 import jax.numpy as jnp
 from jax import lax
 from jax.sharding import PartitionSpec as P
+from jax.lax import all_gather
 
 TILE = 128
 RIM = 8
@@ -114,7 +115,7 @@
     picked = jnp.take_along_axis(layered, index_grid, axis=1)
     partial_pairs = picked.reshape(gene_count, local_tile.shape[1] * TILE)
     share_width = partial_pairs.shape[1] // lax.axis_size("donor")
-    summed = lax.psum(partial_pairs, "donor")
+    summed = all_gather(partial_pairs, axis_name="donor").sum(axis=0)
     own_pairs = lax.dynamic_slice_in_dim(
         summed, lax.axis_index("donor") * share_width, share_width, 1
     )

time: 696 us -> 664 us (0.954)
  waiting for transfers between devices: 375 us -> 355 us
  between operations: 14.2 us -> 0.79 us
    psum x1 -> x0, waiting for transfers between devices: 20.2 us -> none  [shards(): summed = lax.psum(partial_pairs, 'donor')]
  transfers between devices with their start and end apart: 3 -> 2, of which waited for: 2 -> 1; matrix products, arithmetic and copies ran while one was open for 0% -> 0% of each run, Pallas kernels for 0% -> 0%
where the time goes in v1:
time: 664 us; the launch traced here: 663 us
  waiting for transfers between devices  355 us (53%)
  local copies, waits for them, and re-layouts  260 us (39%)
  other arithmetic  21.1 us (3%)
  matrix products  11.8 us (2%)
  starting transfers between devices  9.24 us (1%)
    ppermute x1, waiting for transfers between devices, with_halo(): before = lax.ppermute(last, axis, up)  355 us
    gather x1, local copies, waits for them, and re-layouts, shards(): picked = jnp.take_along_axis(layered, index_grid, axis=1)  259 us
  transfers between devices with their start and end apart: 2, of which 1 were waited for; matrix products, arithmetic and copies ran while one was open for 0% of the time, Pallas kernels for 0%

profile of v1, /device:TPU:0, one launch (start us, length us, event | category | flops | bytes accessed | tf_op | source)
XLA Modules:
  0.0 662.7 jit_solution(5264704266022263820)
XLA Ops:
  0.6 6.0 convert_reduce_fusion
  6.6 0.2 convert_reduce_fusion.1
  6.8 2.6 all-reduce
  9.5 11.0 %fusion.9 = bf16[1024,4096]{1,0:T(8,128)(2,1)} fusion(bf16[1024,4096]{1,0:T(8,128)(2,1)} %param.5, f32[1024]{0:T(1024)S(1)} %get-tuple-element.298, f32[1024]{0:T(1024)S(1)} %get-tuple-element.297), kind=kLoop, calls=%fused_computation.46 | loop fusion | flops 16777216 | bytes 16785408 | tf_op jit(solution)/shard_map/convert_element_type | solution.py:43
  20.5 8.0 %collective-permute-start = (bf16[1024,4096]{1,0:T(8,128)(2,1)}, bf16[1024,4096]{1,0:T(8,128)(2,1)}, u32[]{:S(2)}, u32[]{:S(2)}) collective-permute-start(bf16[1024,4096]{1,0:T(8,128)(2,1)} %fusion.9), channel_id=1, source_target_pairs={{0,2},{2,4},{4,6},{6,8},{8,10},{10,12},{12,14},{1,3},{3,5},{5,7},{... | collective-permute-start | bytes 25165832 | tf_op jit(solution)/shard_map/ppermute | solution.py:20
  28.5 1.3 collective-permute-start.1
  29.9 0.1 copy.18
  30.0 0.1 copy.17
  30.1 0.2 or_bitcast_fusion
  30.3 355.1 %collective-permute-done = bf16[1024,4096]{1,0:T(8,128)(2,1)} collective-permute-done((bf16[1024,4096]{1,0:T(8,128)(2,1)}, bf16[1024,4096]{1,0:T(8,128)(2,1)}, u32[]{:S(2)}, u32[]{:S(2)}) %collective-permute-start) | collective-permute-done | bytes 8388640 | tf_op jit(solution)/shard_map/ppermute | solution.py:20
  385.4 11.8 %fusion.11 = f32[4,8,24,128]{3,1,2,0:T(8,128)S(1)} fusion(bf16[1024,4096]{1,0:T(8,128)(2,1)} %collective-permute-done.1, bf16[1024,4096]{1,0:T(8,128)(2,1)} %fusion.9, bf16[1024,4096]{1,0:T(8,128)(2,1)} %collective-permute-done, bf16[32,4096]{1,0:T(8,128)(2,1)S(1)} %copy-done.1, f32[32]{0:T(128)S(1)} %get-tuple-element.300, f32[32]{0:T(128)S(1)} %get-tuple-element.299), kind=kOutput, calls=%fused_computation.48 | convolution fusion | flops 881328128 | bytes 25821440 | tf_op jit(solution)/shard_map/dot_general | solution.py:47
  397.3 259.4 %gather_fusion = f32[32768]{0:T(1024)S(1)} fusion(f32[32,24,128]{2,1,0:T(8,128)S(1)} %bitcast.7, s32[32768]{0:T(1024)S(1)} %or_bitcast_fusion), kind=kCustom, calls=%fused_computation | custom fusion | bytes 655360 | tf_op jit(solution)/shard_map/jit(take_along_axis)/gather | solution.py:115
  656.7 0.2 bitcast_select_fusion
  656.9 2.0 all_gather.3
  659.0 3.0 while.21
  659.0 0.3 multiply_multiply_fusion.10
  659.4 0.3 multiply_multiply_fusion.10
  659.8 0.3 multiply_multiply_fusion.10
  660.1 0.3 multiply_multiply_fusion.10
  660.5 0.3 multiply_multiply_fusion.10
  660.9 0.3 multiply_multiply_fusion.10
  661.3 0.3 multiply_multiply_fusion.10
  661.6 0.3 multiply_multiply_fusion.10
  662.0 0.7 subtract_select_fusion
  (19 shorter events, 0.3 us)
Async XLA Ops:
  0.6 6.0 copy-start.1
  9.5 20.3 %copy-start.2 = (s32[32,8]{0,1:T(8,128)S(1)}, s32[32,8]{0,1:T(8,128)}, u32[]{:S(2)}) copy-start(s32[32,8]{0,1:T(8,128)} %param.7) | copy-start | bytes 3076
  20.5 364.8 %collective-permute-start = (bf16[1024,4096]{1,0:T(8,128)(2,1)}, bf16[1024,4096]{1,0:T(8,128)(2,1)}, u32[]{:S(2)}, u32[]{:S(2)}) collective-permute-start(bf16[1024,4096]{1,0:T(8,128)(2,1)} %fusion.9), channel_id=1, source_target_pairs={{0,2},{2,4},{4,6},{6,8},{8,10},{10,12},{12,14},{1,3},{3,5},{5,7},{... | collective-permute-start | bytes 25165832 | tf_op jit(solution)/shard_map/ppermute | solution.py:20
  28.5 356.9 %collective-permute-start.1 = (bf16[1024,4096]{1,0:T(8,128)(2,1)}, bf16[1024,4096]{1,0:T(8,128)(2,1)}, u32[]{:S(2)}, u32[]{:S(2)}) collective-permute-start(bf16[1024,4096]{1,0:T(8,128)(2,1)} %fusion.9), channel_id=1, source_target_pairs={{2,0},{4,2},{6,4},{8,6},{10,8},{12,10},{14,12},{3,1},{5,3},{7,5},{... | collective-permute-start | bytes 25165832 | tf_op jit(solution)/shard_map/ppermute | solution.py:21
  658.9 3.8 copy-start
